TPU v7x, 256 devices: a whole 4x4x8 slice. The times are simulated.
256 devices in a mesh: section: 4 (over z_lo), rep: 8 (over y, core), tp: 8 (over z_hi, x).
Axes of the slice: x: 4, y: 4, z: 8 (z_hi: 2, z_lo: 4; z = z_hi * 4 + z_lo), core: 2. Of those that a mesh axis runs over, the one named last changes fastest.
Arguments:
- acts: bfloat16 [8, 256, 896], P('rep', None, 'tp'), may hold values from -6 to 6
- cotangent: bfloat16 [8, 256, 896], P('rep', None, 'tp'), may hold values from -8.5 to 8.5
- w_gate: bfloat16 [4, 8, 896, 4864], P('section', 'rep', None, 'tp'), may hold values from -3 to 3
- w_up: bfloat16 [4, 8, 896, 4864], P('section', 'rep', None, 'tp'), may hold values from -3 to 3
- w_down: bfloat16 [4, 8, 4864, 896], P('section', 'rep', 'tp'), may hold values from -4.2 to 4.2
- m_gate: bfloat16 [4, 8, 896, 4864], P('section', 'rep', None, 'tp'), may hold values from -0.099609375 to 0.099609375
- m_up: bfloat16 [4, 8, 896, 4864], P('section', 'rep', None, 'tp'), may hold values from -0.099609375 to 0.099609375
- m_down: bfloat16 [4, 8, 4864, 896], P('section', 'rep', 'tp'), may hold values from -0.099609375 to 0.099609375
- v_gate: bfloat16 [4, 8, 896, 4864], P('section', 'rep', None, 'tp'), may hold values from 0.0009994507 to 0.099609375
- v_up: bfloat16 [4, 8, 896, 4864], P('section', 'rep', None, 'tp'), may hold values from 0.0009994507 to 0.099609375
- v_down: bfloat16 [4, 8, 4864, 896], P('section', 'rep', 'tp'), may hold values from 0.0009994507 to 0.099609375
- steps: int32 [4], P('section'), may hold values from 0 to 999
Outputs:
- section_out: bfloat16 [4, 8, 256, 896], P('section', 'rep', None, 'tp')
- section_in_grad: bfloat16 [4, 8, 256, 896], P('section', 'rep', None, 'tp')
- new_gate: bfloat16 [4, 8, 896, 4864], P('section', 'rep', None, 'tp')
- new_up: bfloat16 [4, 8, 896, 4864], P('section', 'rep', None, 'tp')
- new_down: bfloat16 [4, 8, 4864, 896], P('section', 'rep', 'tp')
All inputs are finite; a program needn't handle non-finite values.
Results may differ from a plain program's by a relative error of at most 0.023.
Values may be sent and summed in bfloat16 or wider, within the bound.
A program may use at most 128 MiB of HBM per device.

v0:
```python
import functools
import math

import jax
import jax.numpy as jnp
from jax import lax
from jax.experimental import pallas as pl
from jax.experimental.pallas import tpu as pltpu
from jax.sharding import PartitionSpec as P


D = 896
FF = 4864
ROWS = 256
SECTIONS = 4
TP = 8
NX = 4
BLOCK = D // TP
MB = 4
R = ROWS // MB
HALF = ROWS // 2
RELAYED = 448
C = R // NX

NORM_EPS = 1e-06
ADAM_EPS = 1e-08
LEARN = 0.3
BETA_ONE = 0.9
BETA_TWO = 0.95
INV_D = 1.0 / math.sqrt(D)
INV_FF = 1.0 / math.sqrt(FF)
MESH = pl.DeviceIdType.MESH
BF16 = jnp.bfloat16
F32 = jnp.float32

CODES = {name: number for number, name in enumerate("IHMThmtOoDGU-")}


PER_WORD = 5


def plan(text):
    return [CODES[name] * MB + int(mb) for name, mb in zip(text[::2], text[1::2])]


def packed(steps):
    words = [steps[at : at + PER_WORD] for at in range(0, len(steps), PER_WORD)]
    return [sum(step << (6 * place) for place, step in enumerate(word)) for word in words]


START = "I0H0H1M0I1H2M1H3T0M2T1M3T2T3"
RETURN = "O0O1O2O3h0h1m0h2m1h3t0m2t1m3t2"
FIRST = plan(START + "O0O1O2O3h0h1m0h2m1h3m2m3D0G0U0")
MIDDLE = plan(START + RETURN + "t3o0o1o2o3D0G0U0")
FIRST = FIRST + plan("-0") * (len(MIDDLE) - len(FIRST))
TURN = plan("I0I1H0H1M0m0H2M1m1t0H3M2m2t1M3m3t2t3")
LAST = TURN + plan("D0G0U0T0T1T2T3O0O1O2O3o0o1o2o3")
LAST = LAST + plan("-0") * (len(MIDDLE) - len(LAST))


def rms_parts(rows):
    xf = rows.astype(F32)
    rms = jnp.sqrt(jnp.mean(xf * xf, axis=1, keepdims=True) + NORM_EPS)
    return xf, rms


def dot_nn(left, right):
    return lax.dot_general(left, right, (((1,), (0,)), ((), ())), preferred_element_type=F32)


def dot_tn(left, right):
    return lax.dot_general(left, right, (((0,), (0,)), ((), ())), preferred_element_type=F32)


def dot_nt(left, right):
    return lax.dot_general(left, right, (((1,), (1,)), ((), ())), preferred_element_type=F32)


def chain_kernel(
    acts,
    cot,
    wg_hbm,
    wu_hbm,
    wd_hbm,
    mg_hbm,
    mu_hbm,
    md_hbm,
    vg_hbm,
    vu_hbm,
    vd_hbm,
    out_y,
    out_dx,
    out_gate,
    out_up,
    out_part,
    out_rest,
    wg,
    wu,
    wd,
    mg,
    mu,
    md,
    vg,
    vu,
    vd,
    ng,
    nu,
    nd,
    grad,
    xin,
    full,
    hidden_s,
    dgate_s,
    dup_s,
    act_s,
    slope_s,
    spread,
    nb,
    dyb,
    xrow,
    dyrow,
    part_f,
    part_b,
    rs_f,
    rs_b,
    zsend_f,
    zsend_b,
    zrecv_f,
    zrecv_b,
    ost_f,
    ost_b,
    orecv_f,
    orecv_b,
    ost_x,
    orecv_x,
    load_sem,
    store_sem,
    in_send,
    in_recv,
    ag_send,
    ag_recv,
    rs_send,
    rs_recv,
    z_send,
    z_recv,
    o_send,
    o_recv,
):
    s = lax.axis_index("section")
    t = lax.axis_index("tp")
    h = t // NX
    x = t % NX
    own = pl.ds(pl.multiple_of(x * C, C), C)

    def peer_x(k):
        return (x + k) % NX

    loads = [
        pltpu.make_async_copy(src, dst, load_sem.at[number])
        for number, (src, dst) in enumerate(
            (
                (wg_hbm, wg),
                (wu_hbm, wu),
                (wd_hbm, wd),
                (md_hbm, md),
                (vd_hbm, vd),
                (mg_hbm, mg),
                (vg_hbm, vg),
                (mu_hbm, mu),
                (vu_hbm, vu),
            )
        )
    ]
    stores = [
        pltpu.make_async_copy(src, dst, store_sem.at[number])
        for number, (src, dst) in enumerate(
            (
                (nd.at[:RELAYED], out_part),
                (nd.at[RELAYED:], out_rest),
                (ng, out_gate),
                (nu, out_up),
            )
        )
    ]
    for load in loads[:3]:
        load.start()

    barrier = pltpu.get_barrier_semaphore()
    for k in range(1, TP):
        pl.semaphore_signal(barrier, inc=1, device_id={"tp": (t + k) % TP}, device_id_type=MESH)
    for step in (1, SECTIONS - 1):
        for hh in range(2):
            pl.semaphore_signal(
                barrier,
                inc=1,
                device_id={"section": (s + step) % SECTIONS, "tp": hh * NX + x},
                device_id_type=MESH,
            )
    pl.semaphore_wait(barrier, TP - 1 + 4)

    def block_of(who):
        return pl.ds(pl.multiple_of(who * BLOCK, BLOCK), BLOCK)

    def half_of(piece):
        return pl.ds(pl.multiple_of(piece * HALF, HALF), HALF)

    def in_copy(src, piece, k):
        return pltpu.make_async_remote_copy(
            src_ref=src.at[:, half_of(piece)],
            dst_ref=xin.at[block_of(t), half_of(piece)],
            send_sem=in_send.at[piece, k],
            recv_sem=in_recv.at[piece, t],
            device_id={"tp": (t + k) % TP},
            device_id_type=MESH,
        )

    def in_wait(piece, k):
        who = (t + k) % TP
        pltpu.make_async_remote_copy(
            src_ref=xin.at[block_of(who), half_of(piece)],
            dst_ref=xin.at[block_of(who), half_of(piece)],
            send_sem=in_send.at[piece, k],
            recv_sem=in_recv.at[piece, who],
            device_id={"tp": who},
            device_id_type=MESH,
        ).wait_recv()

    order = (4, 5, 3, 6, 2, 7, 1)

    @pl.when(s == 0)
    def _():
        for piece in range(2):
            for k in order:
                in_copy(acts, piece, k).start()

    @pl.when(s == SECTIONS - 1)
    def _():
        for piece in range(2):
            for k in order:
                in_copy(cot, piece, k).start()

    for load in loads[3:]:
        load.start()

    def gather_blocks(src, piece):
        xin[block_of(t), half_of(piece)] = src[:, half_of(piece)]
        for k in range(1, TP):
            in_wait(piece, k)
        full[half_of(piece), :] = xin[:, half_of(piece)].astype(F32).T.astype(BF16)

    def ag_copy(buf, kind, mb, k):
        return pltpu.make_async_remote_copy(
            src_ref=buf.at[mb, own],
            dst_ref=buf.at[mb, own],
            send_sem=ag_send.at[kind, mb, k],
            recv_sem=ag_recv.at[kind, mb, NX - k],
            device_id={"tp": h * NX + peer_x(k)},
            device_id_type=MESH,
        )

    def ag_wait(buf, kind, mb, k):
        rows = pl.ds(pl.multiple_of(peer_x(k) * C, C), C)
        pltpu.make_async_remote_copy(
            src_ref=buf.at[mb, rows],
            dst_ref=buf.at[mb, rows],
            send_sem=ag_send.at[kind, mb, k],
            recv_sem=ag_recv.at[kind, mb, k],
            device_id={"tp": h * NX + peer_x(k)},
            device_id_type=MESH,
        ).wait_recv()

    def rs_copy(part, buf, kind, mb, k):
        rows = pl.ds(pl.multiple_of(peer_x(k) * C, C), C)
        return pltpu.make_async_remote_copy(
            src_ref=part.at[mb, rows],
            dst_ref=buf.at[mb, NX - k],
            send_sem=rs_send.at[kind, mb, k],
            recv_sem=rs_recv.at[kind, mb, NX - k],
            device_id={"tp": h * NX + peer_x(k)},
            device_id_type=MESH,
        )

    def rs_wait(part, buf, kind, mb, k):
        rows = pl.ds(pl.multiple_of(peer_x(k) * C, C), C)
        pltpu.make_async_remote_copy(
            src_ref=part.at[mb, rows],
            dst_ref=buf.at[mb, k],
            send_sem=rs_send.at[kind, mb, k],
            recv_sem=rs_recv.at[kind, mb, k],
            device_id={"tp": h * NX + peer_x(k)},
            device_id_type=MESH,
        ).wait_recv()

    def z_copy(src, buf, kind, mb, hh):
        to = s + 1 if kind == 0 else s - 1
        return pltpu.make_async_remote_copy(
            src_ref=src.at[mb],
            dst_ref=buf.at[mb, h],
            send_sem=z_send.at[kind, mb, hh],
            recv_sem=z_recv.at[kind, mb, h],
            device_id={"section": to % SECTIONS, "tp": hh * NX + x},
            device_id_type=MESH,
        )

    def z_wait(src, buf, kind, mb, hh):
        pltpu.make_async_remote_copy(
            src_ref=src.at[mb],
            dst_ref=buf.at[mb, hh],
            send_sem=z_send.at[kind, mb, hh],
            recv_sem=z_recv.at[kind, mb, hh],
            device_id={"tp": (1 - h) * NX + x},
            device_id_type=MESH,
        ).wait_recv()

    def o_copy(ost, orecv, kind, mb, k):
        who = (t + k) % TP
        return pltpu.make_async_remote_copy(
            src_ref=ost.at[mb, who],
            dst_ref=orecv.at[h, mb, x],
            send_sem=o_send.at[kind, mb, k],
            recv_sem=o_recv.at[kind, mb, TP - k],
            device_id={"tp": who},
            device_id_type=MESH,
        )

    def x_copy(mb, k):
        who = (t + k) % TP
        return pltpu.make_async_remote_copy(
            src_ref=ost_x.at[mb, who],
            dst_ref=orecv_x.at[t, mb],
            send_sem=o_send.at[1, mb, k],
            recv_sem=o_recv.at[1, mb, TP - k],
            device_id={"tp": who},
            device_id_type=MESH,
        )

    def x_wait(mb, k):
        who = (t + k) % TP
        pltpu.make_async_remote_copy(
            src_ref=ost_x.at[mb, who],
            dst_ref=orecv_x.at[who, mb],
            send_sem=o_send.at[1, mb, k],
            recv_sem=o_recv.at[1, mb, k],
            device_id={"tp": who},
            device_id_type=MESH,
        ).wait_recv()

    def o_wait(ost, orecv, kind, mb, k):
        who = (t + k) % TP
        pltpu.make_async_remote_copy(
            src_ref=ost.at[mb, who],
            dst_ref=orecv.at[who // NX, mb, who % NX],
            send_sem=o_send.at[kind, mb, k],
            recv_sem=o_recv.at[kind, mb, k],
            device_id={"tp": who},
            device_id_type=MESH,
        ).wait_recv()

    far_first = (2, 1, 3)

    def step_first(piece):
        @pl.when(piece == 0)
        def _():
            for load in loads[:3]:
                load.wait()

        @pl.when(s == 0)
        def _():
            gather_blocks(acts, piece)
            for b in range(MB // 2):
                mb = piece * (MB // 2) + b
                xf, rms = rms_parts(full[pl.ds(pl.multiple_of(mb * R, R), R), :])
                nb[mb] = (xf / rms).astype(BF16)
                xrow[mb] = full[pl.ds(pl.multiple_of(mb * R + x * C, C), C), :]

        @pl.when(s == SECTIONS - 1)
        def _():
            gather_blocks(cot, piece)
            for b in range(MB // 2):
                mb = piece * (MB // 2) + b
                dyb[mb] = full[pl.ds(pl.multiple_of(mb * R, R), R), :]
                dyrow[mb] = full[pl.ds(pl.multiple_of(mb * R + x * C, C), C), :]

    def head_fwd(mb):
        @pl.when(s > 0)
        def _():
            z_wait(zsend_f, zrecv_f, 0, mb, 0)
            z_wait(zsend_f, zrecv_f, 0, mb, 1)
            rows = (zrecv_f[mb, 0].astype(F32) + zrecv_f[mb, 1].astype(F32)).astype(BF16)
            xrow[mb] = rows
            xf, rms = rms_parts(rows)
            nb[mb, own] = (xf / rms).astype(BF16)
            for k in far_first:
                ag_copy(nb, 0, mb, k).start()

    def main_fwd(mb):
        @pl.when(s > 0)
        def _():
            for k in (1, 3, 2):
                ag_wait(nb, 0, mb, k)

        normed = nb[mb]
        gate = dot_nt(normed, wg[...]) * INV_D
        upper = dot_nt(normed, wu[...]) * INV_D
        sig = jax.nn.sigmoid(gate)
        active = gate * sig
        hidden = (active * upper).astype(BF16)
        part_f[mb] = (dot_nn(hidden, wd[...]) * INV_FF).astype(BF16)
        for k in far_first:
            rs_copy(part_f, rs_f, 0, mb, k).start()
        hidden_s[mb] = hidden
        act_s[mb] = active
        slope_s[mb] = upper * sig * (1.0 + gate * (1.0 - sig))

    def half_sum(part, buf, kind, mb):
        for k in (1, 3, 2):
            rs_wait(part, buf, kind, mb, k)
        total = part[mb, own].astype(F32)
        for k in range(1, NX):
            total = total + buf[mb, k].astype(F32)
        return total

    def tail_fwd(mb):
        half = half_sum(part_f, rs_f, 0, mb)
        zsend_f[mb] = (half + 0.5 * xrow[mb].astype(F32)).astype(BF16)

        @pl.when(s < SECTIONS - 1)
        def _():
            z_copy(zsend_f, zrecv_f, 0, mb, 0).start()
            z_copy(zsend_f, zrecv_f, 0, mb, 1).start()

    def head_bwd(mb):
        @pl.when(s < SECTIONS - 1)
        def _():
            z_wait(zsend_b, zrecv_b, 1, mb, 0)
            z_wait(zsend_b, zrecv_b, 1, mb, 1)
            rows = (zrecv_b[mb, 0].astype(F32) + zrecv_b[mb, 1].astype(F32)).astype(BF16)
            dyrow[mb] = rows
            dyb[mb, own] = rows
            for k in far_first:
                ag_copy(dyb, 1, mb, k).start()

    def main_bwd(mb):
        @pl.when(s < SECTIONS - 1)
        def _():
            for k in (1, 3, 2):
                ag_wait(dyb, 1, mb, k)

        dh = dot_nt(dyb[mb], wd[...]) * INV_FF
        dgate = (dh * slope_s[mb]).astype(BF16)
        dup = (dh * act_s[mb]).astype(BF16)
        part = (dot_nn(dgate, wg[...]) + dot_nn(dup, wu[...])) * INV_D

        @pl.when(s > 0)
        def _():
            part_b[mb] = part.astype(BF16)
            for k in far_first:
                rs_copy(part_b, rs_b, 1, mb, k).start()

        @pl.when(s == 0)
        def _():
            xf, rms = rms_parts(full[pl.ds(pl.multiple_of(mb * R, R), R), :])
            normed = xf / rms
            stat = jnp.sum(part * normed, axis=1, keepdims=True) / D
            share = dyb[mb].astype(F32) * (1.0 / TP) + (part - normed * stat) / rms
            wide = dot_nn(share.astype(BF16), spread[...]).astype(BF16)
            for q in range(TP):
                ost_x[mb, q] = wide[:, q * 128 : (q + 1) * 128]
            orecv_x[t, mb] = ost_x[mb, t]
            for k in order:
                x_copy(mb, k).start()

        dgate_s[mb] = dgate
        dup_s[mb] = dup

    def tail_bwd(mb):
        xf, rms = rms_parts(xrow[mb])
        normed = xf / rms
        half = half_sum(part_b, rs_b, 1, mb)
        stat = jnp.sum(half * normed, axis=1, keepdims=True) / D
        grad = 0.5 * dyrow[mb].astype(F32) + (half - normed * stat) / rms
        zsend_b[mb] = grad.astype(BF16)

        z_copy(zsend_b, zrecv_b, 1, mb, 0).start()
        z_copy(zsend_b, zrecv_b, 1, mb, 1).start()

    def spread_columns(zsend, ost, orecv, kind, mb):
        wide = dot_nn(zsend[mb], spread[...]).astype(BF16)
        for q in range(TP):
            ost[mb, q] = wide[:, q * 128 : (q + 1) * 128]
        orecv[h, mb, x] = ost[mb, t]
        for k in order:
            o_copy(ost, orecv, kind, mb, k).start()

    def out_fwd(mb):
        @pl.when(mb == 0)
        def _():
            feature = lax.broadcasted_iota(jnp.int32, (D, TP * 128), 0)
            place = lax.broadcasted_iota(jnp.int32, (D, TP * 128), 1)
            lane = place % 128
            hit = (feature == (place // 128) * BLOCK + lane) & (lane < BLOCK)
            spread[...] = jnp.where(hit, 1.0, 0.0).astype(BF16)

        spread_columns(zsend_f, ost_f, orecv_f, 0, mb)

    def out_bwd(mb):
        spread_columns(zsend_b, ost_b, orecv_b, 1, mb)

    def update(number, units, rows, scale, weight, first, second, new):
        loads[3 + 2 * number].wait()
        loads[4 + 2 * number].wait()
        hid = weight.shape[0]
        grad[...] = dot_tn(units[...].reshape(ROWS, hid), rows[...].reshape(ROWS, D)) * scale

        def piece(index, carry):
            part = pl.ds(pl.multiple_of(index * 32, 32), 32)
            g = grad[part, :]
            m_new = BETA_ONE * first[part, :].astype(F32) + (1.0 - BETA_ONE) * g
            v_new = BETA_TWO * second[part, :].astype(F32) + (1.0 - BETA_TWO) * g * g
            step = LEARN * m_new / (jnp.sqrt(v_new) + ADAM_EPS)
            new[part, :] = (weight[part, :].astype(F32) - step).astype(BF16)
            return carry

        lax.fori_loop(0, hid // 32, piece, 0)
        for store in stores[:2] if number == 0 else stores[number + 1 : number + 2]:
            store.start()

    def update_down(mb):
        update(0, hidden_s, dyb, INV_FF, wd, md, vd, nd)

    def update_gate(mb):
        update(1, dgate_s, nb, INV_D, wg, mg, vg, ng)

    def update_up(mb):
        update(2, dup_s, nb, INV_D, wu, mu, vu, nu)

    def finish():
        def columns(kind, ost, orecv, out):
            for b in range(MB):
                for k in range(1, TP):
                    o_wait(ost, orecv, kind, b, k)
            halves = orecv[...].reshape(2, ROWS, 128).astype(F32)
            out[...] = (halves[0] + halves[1]).T[:BLOCK].astype(BF16)

        columns(0, ost_f, orecv_f, out_y)

        @pl.when(s > 0)
        def _():
            columns(1, ost_b, orecv_b, out_dx)

        @pl.when(s == 0)
        def _():
            for b in range(MB):
                for k in range(1, TP):
                    x_wait(b, k)
            total = orecv_x[0].reshape(ROWS, 128).astype(F32)
            for q in range(1, TP):
                total = total + orecv_x[q].reshape(ROWS, 128).astype(F32)
            out_dx[...] = total.T[:BLOCK].astype(BF16)

    steps = (
        step_first,
        head_fwd,
        main_fwd,
        tail_fwd,
        head_bwd,
        main_bwd,
        tail_bwd,
        out_fwd,
        out_bwd,
        update_down,
        update_gate,
        update_up,
        lambda mb: None,
    )

    words = [
        jnp.where(s == 0, first, jnp.where(s == SECTIONS - 1, last, middle))
        for first, middle, last in zip(packed(FIRST), packed(MIDDLE), packed(LAST))
    ]

    def run(index, carry):
        word = words[0]
        for place in range(1, len(words)):
            word = jnp.where(index // PER_WORD == place, words[place], word)
        step = (word >> (6 * (index % PER_WORD))) & 63
        mb = step % MB
        code = step // MB

        def dispatch(low, high):
            if high - low == 1:
                steps[low](mb)
                return
            middle = (low + high) // 2

            @pl.when(code < middle)
            def _():
                dispatch(low, middle)

            @pl.when(code >= middle)
            def _():
                dispatch(middle, high)

        dispatch(0, len(steps))
        return carry

    lax.fori_loop(0, len(MIDDLE), run, 0)

    for store in stores:
        store.wait()

    @pl.when(s == 0)
    def _():
        for piece in range(2):
            for k in order:
                in_copy(acts, piece, k).wait_send()

    @pl.when(s == SECTIONS - 1)
    def _():
        for piece in range(2):
            for k in order:
                in_copy(cot, piece, k).wait_send()

    def drain(mb, carry):
        for k in far_first:
            rs_copy(part_f, rs_f, 0, mb, k).wait_send()
        for k in range(1, TP):
            o_copy(ost_f, orecv_f, 0, mb, k).wait_send()

        @pl.when(s == 0)
        def _():
            for k in range(1, TP):
                x_copy(mb, k).wait_send()

        @pl.when(s > 0)
        def _():
            for k in far_first:
                ag_copy(nb, 0, mb, k).wait_send()
                rs_copy(part_b, rs_b, 1, mb, k).wait_send()
            for k in range(1, TP):
                o_copy(ost_b, orecv_b, 1, mb, k).wait_send()
            for hh in range(2):
                z_copy(zsend_b, zrecv_b, 1, mb, hh).wait_send()

        @pl.when(s < SECTIONS - 1)
        def _():
            for k in far_first:
                ag_copy(dyb, 1, mb, k).wait_send()
            for hh in range(2):
                z_copy(zsend_f, zrecv_f, 0, mb, hh).wait_send()

        return carry

    lax.fori_loop(0, MB, drain, 0)
    finish()


def chain(acts, cot, weights, firsts, seconds):
    hid = weights[0].shape[0]
    vm = pl.BlockSpec(memory_space=pltpu.VMEM)
    hbm = pl.BlockSpec(memory_space=pl.ANY)
    shape = jax.ShapeDtypeStruct
    dma = pltpu.SemaphoreType.DMA
    return pl.pallas_call(
        chain_kernel,
        out_shape=(shape((BLOCK, ROWS), BF16),) * 2
        + (shape((hid, D), BF16),) * 2
        + (shape((RELAYED, D), BF16), shape((hid - RELAYED, D), BF16)),
        in_specs=[vm] * 2 + [hbm] * 9,
        out_specs=[vm] * 2 + [hbm] * 4,
        scratch_shapes=[pltpu.VMEM((hid, D), BF16)] * 12
        + [
            pltpu.VMEM((hid, D), F32),
            pltpu.VMEM((D, ROWS), BF16),
            pltpu.VMEM((ROWS, D), BF16),
            pltpu.VMEM((MB, R, hid), BF16),
            pltpu.VMEM((MB, R, hid), BF16),
            pltpu.VMEM((MB, R, hid), BF16),
            pltpu.VMEM((MB, R, hid), F32),
            pltpu.VMEM((MB, R, hid), F32),
            pltpu.VMEM((D, TP * 128), BF16),
            pltpu.VMEM((MB, R, D), BF16),
            pltpu.VMEM((MB, R, D), BF16),
            pltpu.VMEM((MB, C, D), BF16),
            pltpu.VMEM((MB, C, D), BF16),
            pltpu.VMEM((MB, R, D), BF16),
            pltpu.VMEM((MB, R, D), BF16),
            pltpu.VMEM((MB, NX, C, D), BF16),
            pltpu.VMEM((MB, NX, C, D), BF16),
            pltpu.VMEM((MB, C, D), BF16),
            pltpu.VMEM((MB, C, D), BF16),
            pltpu.VMEM((MB, 2, C, D), BF16),
            pltpu.VMEM((MB, 2, C, D), BF16),
            pltpu.VMEM((MB, TP, C, 128), BF16),
            pltpu.VMEM((MB, TP, C, 128), BF16),
            pltpu.VMEM((2, MB, NX, C, 128), BF16),
            pltpu.VMEM((2, MB, NX, C, 128), BF16),
            pltpu.VMEM((MB, TP, R, 128), BF16),
            pltpu.VMEM((TP, MB, R, 128), BF16),
            dma((9,)),
            dma((4,)),
            dma((2, TP)),
            dma((2, TP)),
            dma((2, MB, NX)),
            dma((2, MB, NX)),
            dma((2, MB, NX)),
            dma((2, MB, NX)),
            dma((2, MB, 2)),
            dma((2, MB, 2)),
            dma((2, MB, TP)),
            dma((2, MB, TP)),
        ],
        compiler_params=pltpu.CompilerParams(
            collective_id=0, has_side_effects=True, vmem_limit_bytes=56 * 1024 * 1024
        ),
        name="chain",
    )(acts, cot, *weights, *firsts, *seconds)


def mean(own, other):
    return ((own.astype(F32) + other.astype(F32)) * 0.5).astype(BF16)


def mean_down_kernel(part, rest, rest_moved, *moved_and_out):
    *moved, out = moved_and_out
    moved = [way[...].astype(F32) for way in moved]
    out[:RELAYED, :] = ((part[...].astype(F32) + sum(moved)) * 0.5).astype(BF16)
    out[RELAYED:, :] = mean(rest[...], rest_moved[...])


def mean_down(part, rest, rest_moved, *moved):
    vm = pl.BlockSpec(memory_space=pltpu.VMEM)
    rows = part.shape[0] + rest.shape[0]
    return pl.pallas_call(
        mean_down_kernel,
        out_shape=jax.ShapeDtypeStruct((rows, D), BF16),
        in_specs=[vm] * (3 + len(moved)),
        out_specs=vm,
        cost_estimate=pl.CostEstimate(flops=2 * rows * D, bytes_accessed=6 * rows * D, transcendentals=0),
        name="mean_down",
    )(part, rest, rest_moved, *moved)


def gossip(gate, up, rest, part, distance):
    peers = lax.axis_size("rep")
    onward = [(i, (i + distance) % peers) for i in range(peers)]
    back = [(i, (i - 2) % peers) for i in range(peers) if distance == 2 or i % 2]
    if distance > 2:
        moved = [lax.ppermute(part, "rep", onward)]
    else:
        moved = lax.ppermute(part, "rep", back)
        moved = lax.ppermute(moved, "rep", back)
        if distance == 1:
            last = [(i, (i - 3) % peers) for i in range(peers) if i % 2]
            within = [(i, i + 1) for i in range(peers) if i % 2 == 0]
            moved = [lax.ppermute(moved, "rep", last), lax.ppermute(part, "rep", within)]
        else:
            moved = [lax.ppermute(moved, "rep", back)]
    pairs = []
    for own in (gate, rest, up):
        pairs.append((own, lax.ppermute(own, "rep", onward)))
    new_gate, new_up = mean(*pairs[0]), mean(*pairs[2])
    new_down = mean_down(part, *pairs[1], *moved)
    return lax.optimization_barrier((new_gate, new_up, new_down))


def on_device(
    acts, cotangent, w_gate, w_up, w_down, m_gate, m_up, m_down, v_gate, v_up, v_down, steps
):
    def by_units(gate, up, down):
        return gate[0, 0].T, up[0, 0].T, down[0, 0]

    y, dx, gate, up, part, rest = chain(
        acts[0].T,
        cotangent[0].T,
        by_units(w_gate, w_up, w_down),
        by_units(m_gate, m_up, m_down),
        by_units(v_gate, v_up, v_down),
    )
    levels = lax.axis_size("rep").bit_length() - 1
    branches = [functools.partial(gossip, distance=2**level) for level in range(levels)]
    new_gate, new_up, new_down = lax.switch(
        steps[0] % levels, branches, gate, up, rest, part
    )
    return (
        y.T[None, None],
        dx.T[None, None],
        new_gate.T[None, None],
        new_up.T[None, None],
        new_down[None, None],
    )


def solution(mesh):
    return jax.shard_map(
        on_device,
        mesh=mesh,
        in_specs=(
            P("rep", None, "tp"),
            P("rep", None, "tp"),
            P("section", "rep", None, "tp"),
            P("section", "rep", None, "tp"),
            P("section", "rep", "tp", None),
            P("section", "rep", None, "tp"),
            P("section", "rep", None, "tp"),
            P("section", "rep", "tp", None),
            P("section", "rep", None, "tp"),
            P("section", "rep", None, "tp"),
            P("section", "rep", "tp", None),
            P("section"),
        ),
        out_specs=(
            P("section", "rep", None, "tp"),
            P("section", "rep", None, "tp"),
            P("section", "rep", None, "tp"),
            P("section", "rep", None, "tp"),
            P("section", "rep", "tp", None),
        ),
        check_vma=False,
    )
```

profile of v0, /device:TPU:64, one launch (start us, length us, event | category | flops | bytes accessed | tf_op | source)
XLA Modules:
  0.0 171.9 jit_solution(4156686386703354414)
XLA Ops:
  1.3 100.0 %chain.1 = (bf16[112,256]{1,0:T(8,128)(2,1)}, bf16[112,256]{1,0:T(8,128)(2,1)}, bf16[608,896]{1,0:T(8,128)(2,1)S(1)}, bf16[608,896]{1,0:T(8,128)(2,1)S(1)}, bf16...) custom-call(bf16[112,256]{1,0:T(8,128)(2,1)} %bitcast.56, bf16[112,256]{1,0:T(8,128)(2,1)} %bitcast.57, ...), custom_call_target="tpu_custom_call" | custom-call | tf_op jit(solution)/shard_map/chain/pallas_call | solution.py:664
  101.3 67.7 %conditional.1 = (bf16[608,896]{1,0:T(8,128)(2,1)}, bf16[608,896]{1,0:T(8,128)(2,1)S(1)}, bf16[1,1,608,896]{3,2,1,0:T(8,128)(2,1)}) conditional(s32[]{:T(128)} %clamp.3, (bf16[608,896]{1,0:T(8,128)(2,1)S(1)}, bf16[608,896]{1,0:T(8,128)(2,1)S(1)}, bf16[160,896]{1,0:T(8,128)(2,1)S(1)}, bf16[448,896]{1,0:T(8,128)(2,1)S(1)}) %tuple.26, ...), branch_computations={%region_0.1_spmd, %region_1.2_spmd, %region_2.3_spmd} | conditional | flops 6537216 | bytes 36872552 | solution.py:782
  101.5 3.4 %collective-permute-start.13 = (bf16[608,896]{1,0:T(8,128)(2,1)S(1)}, bf16[608,896]{1,0:T(8,128)(2,1)}, u32[]{:S(2)}, u32[]{:S(2)}) collective-permute-start(bf16[608,896]{1,0:T(8,128)(2,1)S(1)} %get-tuple-element.48), channel_id=1, source_target_pairs={{0,32},{8,40},{16,48},{24,56},{32,0},{40,8},{48,16},{56,24},{1,33}... | collective-permute-start | bytes 3268616 | tf_op jit(solution)/shard_map/cond/branch_2_fun/ppermute | solution.py:761
  104.9 0.2 collective-permute-start.16
  105.1 3.3 %collective-permute-start.14 = (bf16[608,896]{1,0:T(8,128)(2,1)S(1)}, bf16[608,896]{1,0:T(8,128)(2,1)}, u32[]{:S(2)}, u32[]{:S(2)}) collective-permute-start(bf16[608,896]{1,0:T(8,128)(2,1)S(1)} %get-tuple-element.49), channel_id=1, source_target_pairs={{0,32},{8,40},{16,48},{24,56},{32,0},{40,8},{48,16},{56,24},{1,33}... | collective-permute-start | bytes 3268616 | tf_op jit(solution)/shard_map/cond/branch_2_fun/ppermute | solution.py:761
  108.4 0.2 collective-permute-start.15
  108.7 52.7 %collective-permute-done.15.rest_moved = bf16[160,896]{1,0:T(8,128)(2,1)S(1)} collective-permute-done((bf16[160,896]{1,0:T(8,128)(2,1)S(1)}, bf16[160,896]{1,0:T(8,128)(2,1)S(1)}, u32[]{:S(2)}, u32[]{:S(2)}) %collective-permute-start.15) | collective-permute-done | bytes 286752 | tf_op jit(solution)/shard_map/cond/branch_2_fun/ppermute | solution.py:761
  161.4 0.0 copy-start.4
  161.4 0.0 collective-permute-done.16.moved_and_out_0_
  161.4 0.7 copy-done.4
  162.1 2.5 %mean_down.5 = bf16[608,896]{1,0:T(8,128)(2,1)} custom-call(bf16[448,896]{1,0:T(8,128)(2,1)S(1)} %get-tuple-element.50.part, bf16[160,896]{1,0:T(8,128)(2,1)S(1)} %get-tuple-element.51.rest, bf16[160,896]{1,0:T(8,128)(2,1)} %copy-done.4, bf16[448,896]{1,0:T(8,128)(2,1)} %collective-permute-done.16.moved_and_out_0_), custom_call_target="tpu_custom_call" | custom-call | flops 1089536 | bytes 3268608 | tf_op jit(solution)/shard_map/cond/branch_2_fun/mean_down/pallas_call | solution.py:734
  164.6 0.0 collective-permute-done.13
  164.6 2.6 %multiply_convert_fusion.5 = bf16[608,896]{1,0:T(8,128)(2,1)} fusion(bf16[608,896]{1,0:T(8,128)(2,1)} %collective-permute-done.13, bf16[608,896]{1,0:T(8,128)(2,1)S(1)} %get-tuple-element.48), kind=kLoop, calls=%fused_computation.5 | loop fusion | flops 2723840 | bytes 3268608 | tf_op jit(solution)/shard_map/cond/branch_2_fun/convert_element_type | solution.py:721
  167.2 0.0 collective-permute-done.14
  167.2 1.6 multiply_convert_fusion.4
  169.0 0.0 copy-start
  169.0 1.5 copy.29
  170.5 1.4 copy.30
  171.9 0.0 copy-done
Async XLA Ops:
  101.5 63.1 %collective-permute-start.13 = (bf16[608,896]{1,0:T(8,128)(2,1)S(1)}, bf16[608,896]{1,0:T(8,128)(2,1)}, u32[]{:S(2)}, u32[]{:S(2)}) collective-permute-start(bf16[608,896]{1,0:T(8,128)(2,1)S(1)} %get-tuple-element.48), channel_id=1, source_target_pairs={{0,32},{8,40},{16,48},{24,56},{32,0},{40,8},{48,16},{56,24},{1,33}... | collective-permute-start | bytes 3268616 | tf_op jit(solution)/shard_map/cond/branch_2_fun/ppermute | solution.py:761
  104.9 56.5 %collective-permute-start.16 = (bf16[448,896]{1,0:T(8,128)(2,1)S(1)}, bf16[448,896]{1,0:T(8,128)(2,1)}, u32[]{:S(2)}, u32[]{:S(2)}) collective-permute-start(bf16[448,896]{1,0:T(8,128)(2,1)S(1)} %get-tuple-element.50.part), channel_id=1, source_target_pairs={{0,32},{8,40},{16,48},{24,56},{32,0},{40,8},{48,16},{56,24},{1,33}... | collective-permute-start | bytes 2408456 | tf_op jit(solution)/shard_map/cond/branch_2_fun/ppermute | solution.py:749
  105.1 62.1 %collective-permute-start.14 = (bf16[608,896]{1,0:T(8,128)(2,1)S(1)}, bf16[608,896]{1,0:T(8,128)(2,1)}, u32[]{:S(2)}, u32[]{:S(2)}) collective-permute-start(bf16[608,896]{1,0:T(8,128)(2,1)S(1)} %get-tuple-element.49), channel_id=1, source_target_pairs={{0,32},{8,40},{16,48},{24,56},{32,0},{40,8},{48,16},{56,24},{1,33}... | collective-permute-start | bytes 3268616 | tf_op jit(solution)/shard_map/cond/branch_2_fun/ppermute | solution.py:761
  108.4 52.9 %collective-permute-start.15 = (bf16[160,896]{1,0:T(8,128)(2,1)S(1)}, bf16[160,896]{1,0:T(8,128)(2,1)S(1)}, u32[]{:S(2)}, u32[]{:S(2)}) collective-permute-start(bf16[160,896]{1,0:T(8,128)(2,1)S(1)} %get-tuple-element.51.rest), channel_id=1, source_target_pairs={{0,32},{8,40},{16,48},{24,56},{32,0},{40,8},{48,16},{56,24},{1,33}... | collective-permute-start | bytes 860168 | tf_op jit(solution)/shard_map/cond/branch_2_fun/ppermute | solution.py:761
  161.4 0.7 copy-start.4
  169.0 3.0 %copy-start = (bf16[608,896]{1,0:T(8,128)(2,1)}, bf16[608,896]{1,0:T(8,128)(2,1)S(1)}, u32[]{:S(2)}) copy-start(bf16[608,896]{1,0:T(8,128)(2,1)S(1)} %get-tuple-element.76) | copy-start | bytes 3268612
where the time goes:
time: 172 us
  Pallas kernels  103 us (60%)
  waiting for transfers between devices  52.7 us (31%)
  starting transfers between devices  7.15 us (4%)
  other arithmetic  4.14 us (2%)
  local copies, waits for them, and re-layouts  3.65 us (2%)
    pallas_call x1, Pallas kernels, chain(): pl.pallas_call(chain_kernel, out_shape=(shape((BLOCK, ROWS), BF16),) * 2...  100 us
    ppermute x3, waiting for transfers between devices, gossip(): pairs.append((own, lax.ppermute(own, 'rep', onward)))  52.7 us
    ppermute x3, starting transfers between devices, gossip(): pairs.append((own, lax.ppermute(own, 'rep', onward)))  6.92 us
    convert_element_type x2, other arithmetic, mean(): return ((own.astype(F32) + other.astype(F32)) * 0.5).astype(BF16)  4.14 us
  transfers between devices with their start and end apart: 4, of which 1 were waited for; matrix products, arithmetic and copies ran while one was open for 1% of the time, Pallas kernels for 1%

commit v1 on v0

--- a/solution.py
+++ b/solution.py
@@ -19,7 +19,7 @@
 MB = 4
 R = ROWS // MB
 HALF = ROWS // 2
-RELAYED = 448
+RELAYED = 416
 C = R // NX
 
 NORM_EPS = 1e-06
@@ -540,7 +540,7 @@
                 for k in range(1, TP):
                     o_wait(ost, orecv, kind, b, k)
             halves = orecv[...].reshape(2, ROWS, 128).astype(F32)
-            out[...] = (halves[0] + halves[1]).T[:BLOCK].astype(BF16)
+            out[...] = (halves[0] + halves[1]).T[:BLOCK]
 
         columns(0, ost_f, orecv_f, out_y)
 
@@ -556,7 +556,7 @@
             total = orecv_x[0].reshape(ROWS, 128).astype(F32)
             for q in range(1, TP):
                 total = total + orecv_x[q].reshape(ROWS, 128).astype(F32)
-            out_dx[...] = total.T[:BLOCK].astype(BF16)
+            out_dx[...] = total.T[:BLOCK]
 
     steps = (
         step_first,
@@ -663,7 +663,7 @@
     dma = pltpu.SemaphoreType.DMA
     return pl.pallas_call(
         chain_kernel,
-        out_shape=(shape((BLOCK, ROWS), BF16),) * 2
+        out_shape=(shape((BLOCK, ROWS), F32),) * 2
         + (shape((hid, D), BF16),) * 2
         + (shape((RELAYED, D), BF16), shape((hid - RELAYED, D), BF16)),
         in_specs=[vm] * 2 + [hbm] * 9,
@@ -783,8 +783,8 @@
         steps[0] % levels, branches, gate, up, rest, part
     )
     return (
-        y.T[None, None],
-        dx.T[None, None],
+        y.astype(BF16).T[None, None],
+        dx.astype(BF16).T[None, None],
         new_gate.T[None, None],
         new_up.T[None, None],
         new_down[None, None],

time: 172 us -> 172 us (level)
  the two profiles are of different devices: /device:TPU:64 before, /device:TPU:72 now
where the time goes in v1:
time: 172 us
  Pallas kernels  103 us (60%)
  waiting for transfers between devices  52.6 us (31%)
  starting transfers between devices  7.06 us (4%)
  other arithmetic  5.73 us (3%)
    pallas_call x1, Pallas kernels, chain(): pl.pallas_call(chain_kernel, out_shape=(shape((BLOCK, ROWS), F32),) * 2 +...  100 us
    ppermute x3, waiting for transfers between devices, gossip(): pairs.append((own, lax.ppermute(own, 'rep', onward)))  52.6 us
    ppermute x3, starting transfers between devices, gossip(): pairs.append((own, lax.ppermute(own, 'rep', onward)))  4.96 us
    convert_element_type x2, other arithmetic, mean(): return ((own.astype(F32) + other.astype(F32)) * 0.5).astype(BF16)  4.13 us
  transfers between devices with their start and end apart: 4, of which 1 were waited for; matrix products, arithmetic and copies ran while one was open for 1% of the time, Pallas kernels for 1%

profile of v1, /device:TPU:72, one launch (start us, length us, event | category | flops | bytes accessed | tf_op | source)
XLA Modules:
  0.0 171.7 jit_solution(14904025665474026010)
XLA Ops:
  1.3 100.5 %chain.1 = (f32[112,256]{1,0:T(8,128)}, f32[112,256]{1,0:T(8,128)}, bf16[608,896]{1,0:T(8,128)(2,1)S(1)}, bf16[608,896]{1,0:T(8,128)(2,1)S(1)}, bf16[416,896]{1,...) custom-call(bf16[112,256]{1,0:T(8,128)(2,1)} %bitcast.56, bf16[112,256]{1,0:T(8,128)(2,1)} %bitcast.57, ...), custom_call_target="tpu_custom_call" | custom-call | tf_op jit(solution)/shard_map/chain/pallas_call | solution.py:664
  101.8 1.6 convert_bitcast_fusion
  103.4 67.3 %conditional.1 = (bf16[608,896]{1,0:T(8,128)(2,1)}, bf16[608,896]{1,0:T(8,128)(2,1)S(1)}, bf16[1,1,608,896]{3,2,1,0:T(8,128)(2,1)}) conditional(s32[]{:T(128)} %clamp.3, (bf16[608,896]{1,0:T(8,128)(2,1)S(1)}, bf16[608,896]{1,0:T(8,128)(2,1)S(1)}, bf16[192,896]{1,0:T(8,128)(2,1)S(1)}, bf16[416,896]{1,0:T(8,128)(2,1)S(1)}) %tuple.26, ...), branch_computations={%region_0.1_spmd, %region_1.2_spmd, %region_2.3_spmd} | conditional | flops 6537216 | bytes 36184424 | solution.py:782
  103.4 2.1 %collective-permute-start.13 = (bf16[608,896]{1,0:T(8,128)(2,1)S(1)}, bf16[608,896]{1,0:T(8,128)(2,1)}, u32[]{:S(2)}, u32[]{:S(2)}) collective-permute-start(bf16[608,896]{1,0:T(8,128)(2,1)S(1)} %get-tuple-element.48), channel_id=1, source_target_pairs={{0,32},{8,40},{16,48},{24,56},{32,0},{40,8},{48,16},{56,24},{1,33}... | collective-permute-start | bytes 3268616 | tf_op jit(solution)/shard_map/cond/branch_2_fun/ppermute | solution.py:761
  105.5 1.4 collective-permute-start.14
  106.9 2.1 %collective-permute-start.16 = (bf16[416,896]{1,0:T(8,128)(2,1)S(1)}, bf16[416,896]{1,0:T(8,128)(2,1)}, u32[]{:S(2)}, u32[]{:S(2)}) collective-permute-start(bf16[416,896]{1,0:T(8,128)(2,1)S(1)} %get-tuple-element.50.part), channel_id=1, source_target_pairs={{0,32},{8,40},{16,48},{24,56},{32,0},{40,8},{48,16},{56,24},{1,33}... | collective-permute-start | bytes 2236424 | tf_op jit(solution)/shard_map/cond/branch_2_fun/ppermute | solution.py:749
  109.0 1.4 collective-permute-start.15
  110.5 52.6 %collective-permute-done.15.rest_moved = bf16[192,896]{1,0:T(8,128)(2,1)S(1)} collective-permute-done((bf16[192,896]{1,0:T(8,128)(2,1)S(1)}, bf16[192,896]{1,0:T(8,128)(2,1)S(1)}, u32[]{:S(2)}, u32[]{:S(2)}) %collective-permute-start.15) | collective-permute-done | bytes 344096 | tf_op jit(solution)/shard_map/cond/branch_2_fun/ppermute | solution.py:761
  163.0 0.0 copy-start.3
  163.0 0.7 copy-done.3
  163.8 0.0 collective-permute-done.16.moved_and_out_0_
  163.8 2.5 %mean_down.5 = bf16[608,896]{1,0:T(8,128)(2,1)} custom-call(bf16[416,896]{1,0:T(8,128)(2,1)S(1)} %get-tuple-element.50.part, bf16[192,896]{1,0:T(8,128)(2,1)S(1)} %get-tuple-element.51.rest, bf16[192,896]{1,0:T(8,128)(2,1)} %copy-done.3, bf16[416,896]{1,0:T(8,128)(2,1)} %collective-permute-done.16.moved_and_out_0_), custom_call_target="tpu_custom_call" | custom-call | flops 1089536 | bytes 3268608 | tf_op jit(solution)/shard_map/cond/branch_2_fun/mean_down/pallas_call | solution.py:734
  166.3 0.0 collective-permute-done.13
  166.3 2.5 %multiply_convert_fusion.5 = bf16[608,896]{1,0:T(8,128)(2,1)} fusion(bf16[608,896]{1,0:T(8,128)(2,1)} %collective-permute-done.13, bf16[608,896]{1,0:T(8,128)(2,1)S(1)} %get-tuple-element.48), kind=kLoop, calls=%fused_computation.5 | loop fusion | flops 2723840 | bytes 3268608 | tf_op jit(solution)/shard_map/cond/branch_2_fun/convert_element_type | solution.py:721
  168.9 0.0 collective-permute-done.14
  168.9 1.6 multiply_convert_fusion.4
  170.7 0.0 copy-start
  170.7 1.0 copy-done
Async XLA Ops:
  103.4 62.9 %collective-permute-start.13 = (bf16[608,896]{1,0:T(8,128)(2,1)S(1)}, bf16[608,896]{1,0:T(8,128)(2,1)}, u32[]{:S(2)}, u32[]{:S(2)}) collective-permute-start(bf16[608,896]{1,0:T(8,128)(2,1)S(1)} %get-tuple-element.48), channel_id=1, source_target_pairs={{0,32},{8,40},{16,48},{24,56},{32,0},{40,8},{48,16},{56,24},{1,33}... | collective-permute-start | bytes 3268616 | tf_op jit(solution)/shard_map/cond/branch_2_fun/ppermute | solution.py:761
  105.5 63.4 %collective-permute-start.14 = (bf16[608,896]{1,0:T(8,128)(2,1)S(1)}, bf16[608,896]{1,0:T(8,128)(2,1)}, u32[]{:S(2)}, u32[]{:S(2)}) collective-permute-start(bf16[608,896]{1,0:T(8,128)(2,1)S(1)} %get-tuple-element.49), channel_id=1, source_target_pairs={{0,32},{8,40},{16,48},{24,56},{32,0},{40,8},{48,16},{56,24},{1,33}... | collective-permute-start | bytes 3268616 | tf_op jit(solution)/shard_map/cond/branch_2_fun/ppermute | solution.py:761
  106.9 56.8 %collective-permute-start.16 = (bf16[416,896]{1,0:T(8,128)(2,1)S(1)}, bf16[416,896]{1,0:T(8,128)(2,1)}, u32[]{:S(2)}, u32[]{:S(2)}) collective-permute-start(bf16[416,896]{1,0:T(8,128)(2,1)S(1)} %get-tuple-element.50.part), channel_id=1, source_target_pairs={{0,32},{8,40},{16,48},{24,56},{32,0},{40,8},{48,16},{56,24},{1,33}... | collective-permute-start | bytes 2236424 | tf_op jit(solution)/shard_map/cond/branch_2_fun/ppermute | solution.py:749
  109.0 54.0 %collective-permute-start.15 = (bf16[192,896]{1,0:T(8,128)(2,1)S(1)}, bf16[192,896]{1,0:T(8,128)(2,1)S(1)}, u32[]{:S(2)}, u32[]{:S(2)}) collective-permute-start(bf16[192,896]{1,0:T(8,128)(2,1)S(1)} %get-tuple-element.51.rest), channel_id=1, source_target_pairs={{0,32},{8,40},{16,48},{24,56},{32,0},{40,8},{48,16},{56,24},{1,33}... | collective-permute-start | bytes 1032200 | tf_op jit(solution)/shard_map/cond/branch_2_fun/ppermute | solution.py:761
  163.0 0.7 copy-start.3
  170.7 1.0 copy-start
